TPU v7x, 32 devices: a whole 2x2x4 slice. The times are simulated.
32 devices in a mesh: section: 2 (over core), seq: 16 (over z, y, x).
Axes of the slice: x: 2, y: 2, z: 4, core: 2. Of those that a mesh axis runs over, the one named last changes fastest.
Arguments:
- tokens: bfloat16 [1, 2048, 1024], P(None, 'seq'), may hold values from -24 to 24
- neighbor_ids: int32 [16, 9], P('seq'), may hold values from 0 to 15, as said below
- neighbor_count: int32 [16], P('seq'), may hold values from 1 to 9, as said below
- w_query: bfloat16 [2, 1024, 1024], P('section')
- w_key: bfloat16 [2, 1024, 1024], P('section')
- w_value: bfloat16 [2, 1024, 1024], P('section'), may hold values from -0.1875 to 0.1875
- w_out: bfloat16 [2, 1024, 1024], P('section'), may hold values from -0.1875 to 0.1875
- norm_gain: float32 [2, 1024], P('section'), may hold values from 0.5 to 3
- w_up: bfloat16 [2, 4096, 1024], P('section', 'seq'), may hold values from -0.1875 to 0.1875
- w_down: bfloat16 [2, 4096, 1024], P('section', 'seq'), may hold values from -0.09375 to 0.09375
- mlp_gain: float32 [2, 1024], P('section'), may hold values from 0.5 to 2
Outputs:
- layer_outputs: bfloat16 [2, 1, 2048, 1024], P('section', None, 'seq')
Inputs may be any that keep to these rules, and one draw needn't show every extreme that they name: `neighbor_ids`: blocks lie row by row on a map 4 blocks wide. Row b lists in its first neighbor_count[b] entries distinct blocks among b and the up to eight blocks beside it on the map (diagonals included), b first; its other entries equal b. `neighbor_count`: some block has 9.
All inputs are finite; a program needn't handle non-finite values.
Results may differ from a plain program's by a relative error of at most 0.017.
Values may be sent and summed in bfloat16 or wider, within the bound.
A program may use at most 128 MiB of HBM per device.

v0:
```python
import math
import jax
import jax.numpy as jnp
from jax import lax
from jax.sharding import PartitionSpec as P

HEADS = 16
BLK = 128
ROW = 4


def from_behind(block, axis, distance):
    devices = range(lax.axis_size(axis))
    route = [(i - distance, i) for i in devices if i - distance in devices]
    return lax.ppermute(block, axis, route)


def fetch_band(packed, reach_count):
    blocks_here = packed.shape[0]
    distances = [0, 1, -1, ROW - 1, 1 - ROW, ROW, -ROW, ROW + 1, -ROW - 1]
    wanted = set(
        (
            (position + jump_size) // blocks_here
            for position in range(blocks_here)
            for jump_size in distances
        )
    )
    pieces = []
    for offset in range(-reach_count, reach_count + 1):
        if offset == 0:
            pieces.append(packed)
        elif offset in wanted:
            pieces.append(from_behind(packed, "seq", -offset))
        else:
            pieces.append(jnp.zeros_like(packed))
    return jnp.concatenate(pieces, axis=0)


def soft_weights(scores, live, score_scale):
    scaled = jnp.where(live, scores * score_scale, -jnp.inf)
    row_max = jnp.max(scaled, axis=-1, keepdims=True)
    exponent = jnp.exp(scaled - row_max)
    return (exponent / jnp.sum(exponent, axis=-1, keepdims=True)).astype(jnp.bfloat16)


def rms_normed(widened, gain):
    return (
        widened * lax.rsqrt(jnp.mean(widened * widened, axis=-1, keepdims=True) + 1e-05) * gain
    ).astype(jnp.bfloat16)


def prepare(inputs, gain, query_weight, key_weight, value_weight):
    tok_rows, width = inputs.shape
    normed = rms_normed(inputs.astype(jnp.float32), gain)
    queries = jnp.dot(normed, query_weight, preferred_element_type=jnp.float32).astype(jnp.bfloat16)
    keys = jnp.dot(normed, key_weight, preferred_element_type=jnp.float32).astype(jnp.bfloat16)
    values = jnp.dot(normed, value_weight, preferred_element_type=jnp.float32).astype(jnp.bfloat16)
    packed = jnp.concatenate([keys, values], axis=-1).reshape(tok_rows // BLK, BLK, 2 * width)
    return (queries, packed)


def finish(
    inputs,
    queries,
    band_rows,
    neighbor_ids,
    neighbor_count,
    out_weight,
    up_weight,
    down_weight,
    second_gain,
    device,
    reach_count,
):
    tok_rows, width = inputs.shape
    blocks_here = tok_rows // BLK
    slot_total = neighbor_ids.shape[1]
    head_size = width // HEADS
    score_scale = 1.0 / math.sqrt(head_size)
    band_start = (device - reach_count) * blocks_here
    slot_live = jnp.arange(slot_total, dtype=jnp.int32)[None, :] < neighbor_count[:, None]
    query_blocks = queries.reshape(blocks_here, BLK, HEADS, head_size)
    band_keys = band_rows[..., :width]
    band_values = band_rows[..., width:]
    local_ids = neighbor_ids - band_start
    key_set = jnp.take(band_keys, local_ids, axis=0).reshape(
        blocks_here, slot_total * BLK, HEADS, head_size
    )
    value_set = jnp.take(band_values, local_ids, axis=0).reshape(
        blocks_here, slot_total * BLK, HEADS, head_size
    )
    key_live = jnp.repeat(slot_live, BLK, axis=1)
    scores = jnp.einsum(
        "bqhd,bkhd->bhqk", query_blocks, key_set, preferred_element_type=jnp.float32
    )
    probs = soft_weights(scores, key_live[:, None, None, :], score_scale)
    mixed = jnp.einsum(
        "bhqk,bkhd->bqhd", probs, value_set, preferred_element_type=jnp.float32
    ).astype(jnp.bfloat16)
    mixed = mixed.reshape(tok_rows, width)
    attended = (
        inputs.astype(jnp.float32) + jnp.dot(mixed, out_weight, preferred_element_type=jnp.float32)
    ).astype(jnp.bfloat16)
    attended_wide = attended.astype(jnp.float32)
    second = rms_normed(attended_wide, second_gain)
    upper_rows = lax.dot_general(
        second, up_weight, (((1,), (1,)), ((), ())), preferred_element_type=jnp.float32
    )
    hidden = jax.nn.gelu(upper_rows, approximate=True).astype(jnp.bfloat16)
    return (
        attended_wide + jnp.dot(hidden, down_weight, preferred_element_type=jnp.float32)
    ).astype(jnp.bfloat16)


def local(
    tokens,
    neighbor_ids,
    neighbor_count,
    w_query,
    w_key,
    w_value,
    w_out,
    norm_gain,
    w_up,
    w_down,
    mlp_gain,
):
    graphs, tok_rows, width = tokens.shape
    blocks_here = tok_rows // BLK
    reach_count = (ROW + blocks_here) // blocks_here
    sections = lax.axis_size("section")
    section_index = lax.axis_index("section")
    device = lax.axis_index("seq")
    ticks = graphs + sections - 1
    up_whole, down_whole = (
        lax.all_gather(w_up, "seq", axis=1, tiled=True),
        lax.all_gather(w_down, "seq", axis=1, tiled=True),
    )
    results = jnp.zeros((1, graphs, tok_rows, width), jnp.bfloat16)
    incoming = jnp.zeros((tok_rows, width), jnp.bfloat16)
    for tick_index in range(ticks):
        first_input = tokens[min(tick_index, graphs - 1)]
        layer_input = jnp.where(section_index == 0, first_input, incoming)
        graph_index = tick_index - section_index
        active = (graph_index >= 0) & (graph_index < graphs)

        def run_prepare(operand_rows):
            return prepare(operand_rows, norm_gain[0], w_query[0], w_key[0], w_value[0])

        def skip_prepare(operand_rows):
            return (
                jnp.zeros((tok_rows, width), jnp.bfloat16),
                jnp.zeros((blocks_here, BLK, 2 * width), jnp.bfloat16),
            )

        queries, packed = lax.cond(active, run_prepare, skip_prepare, layer_input)
        band_rows = fetch_band(packed, reach_count)

        def run_finish(operand_set):
            return finish(
                operand_set[0],
                operand_set[1],
                operand_set[2],
                neighbor_ids,
                neighbor_count,
                w_out[0],
                up_whole[0],
                down_whole[0],
                mlp_gain[0],
                device,
                reach_count,
            )

        def skip_finish(operand_set):
            return jnp.zeros((tok_rows, width), jnp.bfloat16)

        layer_output = lax.cond(active, run_finish, skip_finish, (layer_input, queries, band_rows))
        results = results.at[0, 0].set(jnp.where(graph_index == 0, layer_output, results[0, 0]))
        if tick_index + 1 < ticks:
            incoming = from_behind(layer_output, "section", 1)
    return results


def solution(mesh):
    in_specs = (
        P(None, "seq", None),
        P("seq", None),
        P("seq"),
        P("section", None, None),
        P("section", None, None),
        P("section", None, None),
        P("section", None, None),
        P("section", None),
        P("section", "seq", None),
        P("section", "seq", None),
        P("section", None),
    )
    out_specs = P("section", None, "seq", None)
    return jax.shard_map(local, mesh=mesh, in_specs=in_specs, out_specs=out_specs, check_vma=False)
```

profile of v0, /device:TPU:9, one launch (start us, length us, event | category | flops | bytes accessed | tf_op | source)
XLA Modules:
  0.0 490.4 jit_solution(1373884698683510926)
XLA Ops:
  8.0 1.0 bitcast_select_fusion.5
  9.1 4.2 collective-permute-start
  13.3 3.2 collective-permute-start.1
  16.5 2.8 collective-permute-start.2
  19.3 2.2 collective-permute-start.3
  21.5 4.8 collective-permute-start.4
  26.4 3.0 collective-permute-start.5
  30.2 10.4 %collective-permute-done.1 = bf16[1,128,2048]{2,1,0:T(8,128)(2,1)} collective-permute-done((bf16[1,128,2048]{2,1,0:T(8,128)(2,1)S(1)}, bf16[1,128,2048]{2,1,0:T(8,128)(2,1)}, u32[]{:S(2)}, u32[]{:S(2)}) %collective-permute-start.1) | collective-permute-done | bytes 524320 | tf_op jit(solution)/shard_map/ppermute | solution.py:15
  40.6 1.9 collective-permute-start.6
  42.5 1.9 constant_dynamic-update-slice_fusion.7
  44.4 17.4 %collective-permute-done.2 = bf16[1,128,2048]{2,1,0:T(8,128)(2,1)} collective-permute-done((bf16[1,128,2048]{2,1,0:T(8,128)(2,1)S(1)}, bf16[1,128,2048]{2,1,0:T(8,128)(2,1)}, u32[]{:S(2)}, u32[]{:S(2)}) %collective-permute-start.2) | collective-permute-done | bytes 524320 | tf_op jit(solution)/shard_map/ppermute | solution.py:15
  61.8 1.3 collective-permute-start.7
  63.1 1.9 constant_dynamic-update-slice_fusion.6
  65.9 19.2 %collective-permute-done.3 = bf16[1,128,2048]{2,1,0:T(8,128)(2,1)S(1)} collective-permute-done((bf16[1,128,2048]{2,1,0:T(8,128)(2,1)S(1)}, bf16[1,128,2048]{2,1,0:T(8,128)(2,1)S(1)}, u32[]{:S(2)}, u32[]{:S(2)}) %collective-permute-start.3) | collective-permute-done | bytes 524320 | tf_op jit(solution)/shard_map/ppermute | solution.py:15
  86.7 8.9 %collective-permute-done.4 = bf16[1,128,2048]{2,1,0:T(8,128)(2,1)S(1)} collective-permute-done((bf16[1,128,2048]{2,1,0:T(8,128)(2,1)S(1)}, bf16[1,128,2048]{2,1,0:T(8,128)(2,1)S(1)}, u32[]{:S(2)}, u32[]{:S(2)}) %collective-permute-start.4) | collective-permute-done | bytes 524320 | tf_op jit(solution)/shard_map/ppermute | solution.py:15
  95.6 0.9 constant_dynamic-update-slice_fusion.3
  99.9 67.9 %all-gather.3.cloned.1.call-done = bf16[1,4096,1024]{2,1,0:T(8,128)(2,1)} async-done(((bf16[1,256,1024]{2,1,0:T(8,128)(2,1)}), bf16[1,4096,1024]{2,1,0:T(8,128)(2,1)}) %all-gather.3.cloned.1.call-update) | async-done | bytes 8388624 | tf_op jit(solution)/shard_map/all_gather | solution.py:136
  167.8 113.8 %all-gather.5.cloned.1.call-done = bf16[1,4096,1024]{2,1,0:T(8,128)(2,1)} async-done(((bf16[1,256,1024]{2,1,0:T(8,128)(2,1)}), bf16[1,4096,1024]{2,1,0:T(8,128)(2,1)}) %all-gather.5.cloned.1.call-update) | async-done | bytes 8388624 | tf_op jit(solution)/shard_map/all_gather | solution.py:137
  281.9 1.3 collective-permute-start.8
  283.2 60.4 %collective-permute-done.8 = bf16[128,1024]{1,0:T(8,128)(2,1)S(1)} collective-permute-done((bf16[128,1024]{1,0:T(8,128)(2,1)S(1)}, bf16[128,1024]{1,0:T(8,128)(2,1)S(1)}, u32[]{:S(2)}, u32[]{:S(2)}) %collective-permute-start.8) | collective-permute-done | bytes 262176 | tf_op jit(solution)/shard_map/ppermute | solution.py:15
  343.6 1.0 bitcast_select_fusion.4
  344.6 5.0 %conditional.6 = (bf16[128,1024]{1,0:T(8,128)(2,1)S(1)}, bf16[1,128,2048]{2,1,0:T(8,128)(2,1)S(1)}) conditional(s32[]{:T(128)} %convert_element_type.100, () %tuple.47, (bf16[128,1024]{1,0:T(8,128)(2,1)S(1)}, f32[1,1024]{1,0:T(1,128)S(1)}, bf16[1,1024,1024]{2,1,0:T(8,128)(2,1)}, bf16[1,1024,1024]{2,1,0:T(8,128)(2,1)}, ...), branch_computations={%region_8.10_spmd, %region_9.12_spmd} | conditional | flops 808714368 | bytes 17579052 | solution.py:156
  344.7 2.2 fusion.30
  346.9 2.1 fusion.33
  349.6 4.1 collective-permute-start.9
  353.7 2.1 collective-permute-start.10
  355.8 3.0 collective-permute-start.11
  358.8 2.2 collective-permute-start.12
  361.1 4.9 collective-permute-start.13
  366.0 2.5 collective-permute-start.14
  369.3 3.8 collective-permute-done.10
  373.0 1.9 collective-permute-start.15
  375.8 20.2 %collective-permute-done.11 = bf16[1,128,2048]{2,1,0:T(8,128)(2,1)S(1)} collective-permute-done((bf16[1,128,2048]{2,1,0:T(8,128)(2,1)S(1)}, bf16[1,128,2048]{2,1,0:T(8,128)(2,1)S(1)}, u32[]{:S(2)}, u32[]{:S(2)}) %collective-permute-start.11) | collective-permute-done | bytes 524320 | tf_op jit(solution)/shard_map/ppermute | solution.py:15
  396.0 1.3 collective-permute-start.16
  399.0 18.0 %collective-permute-done.12 = bf16[1,128,2048]{2,1,0:T(8,128)(2,1)S(1)} collective-permute-done((bf16[1,128,2048]{2,1,0:T(8,128)(2,1)S(1)}, bf16[1,128,2048]{2,1,0:T(8,128)(2,1)S(1)}, u32[]{:S(2)}, u32[]{:S(2)}) %collective-permute-start.12) | collective-permute-done | bytes 524320 | tf_op jit(solution)/shard_map/ppermute | solution.py:15
  418.7 1.2 collective-permute-done.13
  419.8 0.9 constant_dynamic-update-slice_fusion.12
  424.1 58.7 %conditional.7 = (bf16[128,1024]{1,0:T(8,128)(2,1)S(1)}) conditional(s32[]{:T(128)} %convert_element_type.100, () %tuple.42, (bf16[128,1024]{1,0:T(8,128)(2,1)S(1)}, bf16[11,128,2048]{2,1,0:T(8,128)(2,1)}, s32[]{:T(128)}, s32[1,9]{1,0:T(1,128)S(1)}, s32[1]{0:T(128)}, /*index=5*/bf16[128,1024]{1,0:T(8,128)(2,1)S(1)}, ...), branch_computations={%region_11.13_spmd, %region_12.17_spmd} | conditional | flops 3047426304 | bytes 114586176 | solution.py:177
  424.8 5.2 %fusion.164 = (bf16[11,128,1024]{2,1,0:T(8,128)(2,1)}, bf16[11,128,1024]{2,1,0:T(8,128)(2,1)S(1)}) fusion(bf16[11,128,2048]{2,1,0:T(8,128)(2,1)} %get-tuple-element.117), kind=kLoop, calls=%fused_computation.169 | loop fusion | bytes 11534336 | tf_op jit(solution)/shard_map/cond/branch_1_fun/slice | solution.py:84
  430.0 4.1 gather_fusion.2
  434.1 2.4 gather_fusion.3
  436.5 4.3 bitcast_select_fusion.3
  440.8 7.3 %reshape.288 = bf16[1152,16,64]{2,1,0:T(8,128)(2,1)} reshape(bf16[1,9,128,1024]{3,2,1,0:T(8,128)(2,1)} %get-tuple-element.189) | data formatting | bytes 4718592 | tf_op jit(solution)/shard_map/reshape.89
  448.3 3.2 fusion.111
  452.3 6.7 %fusion.165 = (f32[16,128]{1,0:T(8,128)S(1)}, f32[16,128,1152]{1,2,0:T(8,128)}) fusion(f32[16,1152,128]{2,1,0:T(8,128)S(1)} %fusion.111, pred[1152]{0:T(1024)(128)(4,1)S(1)} %broadcast_bitcast_fusion.1), kind=kOutput, calls=%fused_computation.170 | output fusion | flops 14156927 | bytes 18883712 | tf_op jit(solution)/shard_map/cond/branch_1_fun/sub | solution.py:42
  459.0 4.7 reshape.287
  463.7 8.2 %fusion.141 = bf16[16,64,128]{2,1,0:T(8,128)(2,1)S(1)} fusion(f32[16,128,1152]{1,2,0:T(8,128)} %get-tuple-element.191, f32[16,128]{1,0:T(8,128)S(1)} %get-tuple-element.190, bf16[1152,16,64]{2,1,0:T(8,128)(2,1)} %reshape.287), kind=kOutput, calls=%fused_computation.123 | convolution fusion | flops 306839552 | bytes 12066816 | tf_op jit(solution)/shard_map/cond/branch_1_fun/bhqk,bkhd->bqhd/dot_general | solution.py:97
  472.5 10.0 %fusion.138 = bf16[128,1024]{1,0:T(8,128)(2,1)S(1)} fusion(f32[128,1024]{1,0:T(8,128)S(1)} %get-tuple-element.193, bf16[1,4096,1024]{2,1,0:T(8,128)(2,1)} %get-tuple-element.125, bf16[1,4096,1024]{2,1,0:T(8,128)(2,1)} %get-tuple-element.124, f32[1024]{0:T(1024)S(1)} %bitcast.180, f32[128]{0:T(128)S(1)} %add_rsqrt_fusion.3), kind=kOutput, calls=%fused_computation.122 | convolution fusion | flops 2152857600 | bytes 17568256 | tf_op jit(solution)/shard_map/cond/branch_1_fun/dot_general | solution.py:111
  (65 shorter events, 20.6 us)
Async XLA Ops:
  6.5 161.2 %all-gather.3.cloned.1.call-start = ((), (), s32[]{:S(2)}) async-start(), calls=%async_computation | async-start | bytes 8912896 | tf_op jit(solution)/shard_map/all_gather | solution.py:136
  7.3 274.3 %all-gather.5.cloned.1.call-start = ((), (), s32[]{:S(2)}) async-start(), calls=%async_computation.1 | async-start | bytes 8912896 | tf_op jit(solution)/shard_map/all_gather | solution.py:137
  9.1 17.3 %collective-permute-start = (bf16[1,128,2048]{2,1,0:T(8,128)(2,1)S(1)}, bf16[1,128,2048]{2,1,0:T(8,128)(2,1)S(1)}, u32[]{:S(2)}, u32[]{:S(2)}) collective-permute-start(bf16[1,128,2048]{2,1,0:T(8,128)(2,1)S(1)} %get-tuple-element.130), channel_id=1, source_target_pairs={{0,5},{1,6},{2,7},{3,8},{4,9},{5,10},{6,11},{7,12},{8,13},{9,14},{... | collective-permute-start | bytes 1572872 | tf_op jit(solution)/shard_map/ppermute | solution.py:15
  13.3 27.3 %collective-permute-start.1 = (bf16[1,128,2048]{2,1,0:T(8,128)(2,1)S(1)}, bf16[1,128,2048]{2,1,0:T(8,128)(2,1)}, u32[]{:S(2)}, u32[]{:S(2)}) collective-permute-start(bf16[1,128,2048]{2,1,0:T(8,128)(2,1)S(1)} %get-tuple-element.130), channel_id=1, source_target_pairs={{0,4},{1,5},{2,6},{3,7},{4,8},{5,9},{6,10},{7,11},{8,12},{9,13},{1... | collective-permute-start | bytes 1572872 | tf_op jit(solution)/shard_map/ppermute | solution.py:15
  16.5 45.4 %collective-permute-start.2 = (bf16[1,128,2048]{2,1,0:T(8,128)(2,1)S(1)}, bf16[1,128,2048]{2,1,0:T(8,128)(2,1)}, u32[]{:S(2)}, u32[]{:S(2)}) collective-permute-start(bf16[1,128,2048]{2,1,0:T(8,128)(2,1)S(1)} %get-tuple-element.130), channel_id=1, source_target_pairs={{0,3},{1,4},{2,5},{3,6},{4,7},{5,8},{6,9},{7,10},{8,11},{9,12},{10... | collective-permute-start | bytes 1572872 | tf_op jit(solution)/shard_map/ppermute | solution.py:15
  19.3 65.8 %collective-permute-start.3 = (bf16[1,128,2048]{2,1,0:T(8,128)(2,1)S(1)}, bf16[1,128,2048]{2,1,0:T(8,128)(2,1)S(1)}, u32[]{:S(2)}, u32[]{:S(2)}) collective-permute-start(bf16[1,128,2048]{2,1,0:T(8,128)(2,1)S(1)} %get-tuple-element.130), channel_id=1, source_target_pairs={{0,1},{1,2},{2,3},{3,4},{4,5},{5,6},{6,7},{7,8},{8,9},{9,10},{10,1... | collective-permute-start | bytes 1572872 | tf_op jit(solution)/shard_map/ppermute | solution.py:15
  21.5 74.1 %collective-permute-start.4 = (bf16[1,128,2048]{2,1,0:T(8,128)(2,1)S(1)}, bf16[1,128,2048]{2,1,0:T(8,128)(2,1)S(1)}, u32[]{:S(2)}, u32[]{:S(2)}) collective-permute-start(bf16[1,128,2048]{2,1,0:T(8,128)(2,1)S(1)} %get-tuple-element.130), channel_id=1, source_target_pairs={{1,0},{2,1},{3,2},{4,3},{5,4},{6,5},{7,6},{8,7},{9,8},{10,9},{11,1... | collective-permute-start | bytes 1572872 | tf_op jit(solution)/shard_map/ppermute | solution.py:15
  26.4 71.0 %collective-permute-start.5 = (bf16[1,128,2048]{2,1,0:T(8,128)(2,1)S(1)}, bf16[1,128,2048]{2,1,0:T(8,128)(2,1)S(1)}, u32[]{:S(2)}, u32[]{:S(2)}) collective-permute-start(bf16[1,128,2048]{2,1,0:T(8,128)(2,1)S(1)} %get-tuple-element.130), channel_id=1, source_target_pairs={{3,0},{4,1},{5,2},{6,3},{7,4},{8,5},{9,6},{10,7},{11,8},{12,9},{13... | collective-permute-start | bytes 1572872 | tf_op jit(solution)/shard_map/ppermute | solution.py:15
  30.2 251.4 %copy-start.10 = (s32[1,9]{1,0:T(1,128)S(1)}, s32[1,9]{1,0:T(1,128)}, u32[]{:S(2)}) copy-start(s32[1,9]{1,0:T(1,128)} %param.26) | copy-start | bytes 112
  30.2 251.4 %copy-start.11 = (f32[1,1024]{1,0:T(1,128)S(1)}, f32[1,1024]{1,0:T(1,128)}, u32[]{:S(2)}) copy-start(f32[1,1024]{1,0:T(1,128)} %param.35) | copy-start | bytes 12292
  40.6 57.6 %collective-permute-start.6 = (bf16[1,128,2048]{2,1,0:T(8,128)(2,1)S(1)}, bf16[1,128,2048]{2,1,0:T(8,128)(2,1)S(1)}, u32[]{:S(2)}, u32[]{:S(2)}) collective-permute-start(bf16[1,128,2048]{2,1,0:T(8,128)(2,1)S(1)} %get-tuple-element.130), channel_id=1, source_target_pairs={{4,0},{5,1},{6,2},{7,3},{8,4},{9,5},{10,6},{11,7},{12,8},{13,9},{1... | collective-permute-start | bytes 1572872 | tf_op jit(solution)/shard_map/ppermute | solution.py:15
  61.8 37.2 %collective-permute-start.7 = (bf16[1,128,2048]{2,1,0:T(8,128)(2,1)S(1)}, bf16[1,128,2048]{2,1,0:T(8,128)(2,1)S(1)}, u32[]{:S(2)}, u32[]{:S(2)}) collective-permute-start(bf16[1,128,2048]{2,1,0:T(8,128)(2,1)S(1)} %get-tuple-element.130), channel_id=1, source_target_pairs={{5,0},{6,1},{7,2},{8,3},{9,4},{10,5},{11,6},{12,7},{13,8},{14,9},{... | collective-permute-start | bytes 1572872 | tf_op jit(solution)/shard_map/ppermute | solution.py:15
  281.6 63.0 %copy-start.8 = (f32[1,1024]{1,0:T(1,128)S(1)}, f32[1,1024]{1,0:T(1,128)}, u32[]{:S(2)}) copy-start(f32[1,1024]{1,0:T(1,128)} %param.32) | copy-start | bytes 12292
  281.8 62.7 %copy-start.4 = (bf16[128,1024]{1,0:T(8,128)(2,1)}, bf16[128,1024]{1,0:T(8,128)(2,1)S(1)}, u32[]{:S(2)}) copy-start(bf16[128,1024]{1,0:T(8,128)(2,1)S(1)} %get-tuple-element.202) | copy-start | bytes 786436
  281.9 61.7 %collective-permute-start.8 = (bf16[128,1024]{1,0:T(8,128)(2,1)S(1)}, bf16[128,1024]{1,0:T(8,128)(2,1)S(1)}, u32[]{:S(2)}, u32[]{:S(2)}) collective-permute-start(bf16[128,1024]{1,0:T(8,128)(2,1)S(1)} %get-tuple-element.202), channel_id=1, source_target_pairs={{0,16},{1,17},{2,18},{3,19},{4,20},{5,21},{6,22},{7,23},{8,24},{9,... | collective-permute-start | bytes 786440 | tf_op jit(solution)/shard_map/ppermute | solution.py:15
  344.6 4.5 copy-start.1
  349.6 16.4 %collective-permute-start.9 = (bf16[1,128,2048]{2,1,0:T(8,128)(2,1)S(1)}, bf16[1,128,2048]{2,1,0:T(8,128)(2,1)S(1)}, u32[]{:S(2)}, u32[]{:S(2)}) collective-permute-start(bf16[1,128,2048]{2,1,0:T(8,128)(2,1)S(1)} %get-tuple-element.132), channel_id=1, source_target_pairs={{0,5},{1,6},{2,7},{3,8},{4,9},{5,10},{6,11},{7,12},{8,13},{9,14},{... | collective-permute-start | bytes 1572872 | tf_op jit(solution)/shard_map/ppermute | solution.py:15
  353.7 19.3 %collective-permute-start.10 = (bf16[1,128,2048]{2,1,0:T(8,128)(2,1)S(1)}, bf16[1,128,2048]{2,1,0:T(8,128)(2,1)S(1)}, u32[]{:S(2)}, u32[]{:S(2)}) collective-permute-start(bf16[1,128,2048]{2,1,0:T(8,128)(2,1)S(1)} %get-tuple-element.132), channel_id=1, source_target_pairs={{0,4},{1,5},{2,6},{3,7},{4,8},{5,9},{6,10},{7,11},{8,12},{9,13},{1... | collective-permute-start | bytes 1572872 | tf_op jit(solution)/shard_map/ppermute | solution.py:15
  355.8 40.2 %collective-permute-start.11 = (bf16[1,128,2048]{2,1,0:T(8,128)(2,1)S(1)}, bf16[1,128,2048]{2,1,0:T(8,128)(2,1)S(1)}, u32[]{:S(2)}, u32[]{:S(2)}) collective-permute-start(bf16[1,128,2048]{2,1,0:T(8,128)(2,1)S(1)} %get-tuple-element.132), channel_id=1, source_target_pairs={{0,3},{1,4},{2,5},{3,6},{4,7},{5,8},{6,9},{7,10},{8,11},{9,12},{10... | collective-permute-start | bytes 1572872 | tf_op jit(solution)/shard_map/ppermute | solution.py:15
  358.8 58.1 %collective-permute-start.12 = (bf16[1,128,2048]{2,1,0:T(8,128)(2,1)S(1)}, bf16[1,128,2048]{2,1,0:T(8,128)(2,1)S(1)}, u32[]{:S(2)}, u32[]{:S(2)}) collective-permute-start(bf16[1,128,2048]{2,1,0:T(8,128)(2,1)S(1)} %get-tuple-element.132), channel_id=1, source_target_pairs={{0,1},{1,2},{2,3},{3,4},{4,5},{5,6},{6,7},{7,8},{8,9},{9,10},{10,1... | collective-permute-start | bytes 1572872 | tf_op jit(solution)/shard_map/ppermute | solution.py:15
  361.1 58.8 %collective-permute-start.13 = (bf16[1,128,2048]{2,1,0:T(8,128)(2,1)S(1)}, bf16[1,128,2048]{2,1,0:T(8,128)(2,1)S(1)}, u32[]{:S(2)}, u32[]{:S(2)}) collective-permute-start(bf16[1,128,2048]{2,1,0:T(8,128)(2,1)S(1)} %get-tuple-element.132), channel_id=1, source_target_pairs={{1,0},{2,1},{3,2},{4,3},{5,4},{6,5},{7,6},{8,7},{9,8},{10,9},{11,1... | collective-permute-start | bytes 1572872 | tf_op jit(solution)/shard_map/ppermute | solution.py:15
  366.0 55.6 %collective-permute-start.14 = (bf16[1,128,2048]{2,1,0:T(8,128)(2,1)S(1)}, bf16[1,128,2048]{2,1,0:T(8,128)(2,1)S(1)}, u32[]{:S(2)}, u32[]{:S(2)}) collective-permute-start(bf16[1,128,2048]{2,1,0:T(8,128)(2,1)S(1)} %get-tuple-element.132), channel_id=1, source_target_pairs={{3,0},{4,1},{5,2},{6,3},{7,4},{8,5},{9,6},{10,7},{11,8},{12,9},{13... | collective-permute-start | bytes 1572872 | tf_op jit(solution)/shard_map/ppermute | solution.py:15
  373.0 49.4 %collective-permute-start.15 = (bf16[1,128,2048]{2,1,0:T(8,128)(2,1)S(1)}, bf16[1,128,2048]{2,1,0:T(8,128)(2,1)S(1)}, u32[]{:S(2)}, u32[]{:S(2)}) collective-permute-start(bf16[1,128,2048]{2,1,0:T(8,128)(2,1)S(1)} %get-tuple-element.132), channel_id=1, source_target_pairs={{4,0},{5,1},{6,2},{7,3},{8,4},{9,5},{10,6},{11,7},{12,8},{13,9},{1... | collective-permute-start | bytes 1572872 | tf_op jit(solution)/shard_map/ppermute | solution.py:15
  396.0 27.2 %collective-permute-start.16 = (bf16[1,128,2048]{2,1,0:T(8,128)(2,1)S(1)}, bf16[1,128,2048]{2,1,0:T(8,128)(2,1)S(1)}, u32[]{:S(2)}, u32[]{:S(2)}) collective-permute-start(bf16[1,128,2048]{2,1,0:T(8,128)(2,1)S(1)} %get-tuple-element.132), channel_id=1, source_target_pairs={{5,0},{6,1},{7,2},{8,3},{9,4},{10,5},{11,6},{12,7},{13,8},{14,9},{... | collective-permute-start | bytes 1572872 | tf_op jit(solution)/shard_map/ppermute | solution.py:15
  424.1 58.7 %copy-start.5 = (bf16[128,1024]{1,0:T(8,128)(2,1)S(1)}, bf16[128,1024]{1,0:T(8,128)(2,1)}, u32[]{:S(2)}) copy-start(bf16[128,1024]{1,0:T(8,128)(2,1)} %copy-done.4) | copy-start | bytes 786436
  424.1 0.7 copy-start.6
  440.8 7.3 %copy-start.7 = (bf16[128,1024]{1,0:T(8,128)(2,1)S(1)}, bf16[128,1024]{1,0:T(8,128)(2,1)}, u32[]{:S(2)}) copy-start(bf16[128,1024]{1,0:T(8,128)(2,1)} %copy-done.6) | copy-start | bytes 786436 | tf_op jit(solution)/shard_map/cond
  463.7 8.2 %copy-start.3 = (bf16[1,1024,1024]{2,1,0:T(8,128)(2,1)S(1)}, bf16[1,1024,1024]{2,1,0:T(8,128)(2,1)}, u32[]{:S(2)}) copy-start(bf16[1,1024,1024]{2,1,0:T(8,128)(2,1)} %get-tuple-element.122) | copy-start | bytes 6291460 | tf_op jit(solution)/shard_map/cond
Sparse Core Ops, SparseCore 0:
  10.1 157.5 all-gather.2
  170.5 111.0 all-gather.4
where the time goes:
time: 491 us; the launch traced here: 490 us
  waiting for transfers between devices  342 us (70%)
  starting transfers between devices  46.8 us (10%)
  local copies, waits for them, and re-layouts  45.5 us (9%)
  matrix products  26.8 us (5%)
  other arithmetic  14.5 us (3%)
  between operations  13.7 us (3%)
    ppermute x17, waiting for transfers between devices, from_behind(): return lax.ppermute(block, axis, route)  159 us
    all_gather x1, waiting for transfers between devices, local(): lax.all_gather(w_down, 'seq', axis=1, tiled=True)  114 us
    all_gather x1, waiting for transfers between devices, local(): lax.all_gather(w_up, 'seq', axis=1, tiled=True)  67.9 us
    ppermute x17, starting transfers between devices, from_behind(): return lax.ppermute(block, axis, route)  46.7 us
    unnamed x30, local copies, waits for them, and re-layouts  19.1 us
    another operation x6, local copies, waits for them, and re-layouts  12.3 us
    dot_general x1, matrix products, finish(): jnp.dot(hidden, down_weight, preferred_element_type=jnp.float32)  10 us
  transfers between devices with their start and end apart: 19, of which 11 were waited for; matrix products, arithmetic and copies ran while one was open for 4% of the time, Pallas kernels for 0%

commit v1 on v0

--- a/solution.py
+++ b/solution.py
@@ -1,12 +1,45 @@
+import functools
 import math
 import jax
 import jax.numpy as jnp
 from jax import lax
 from jax.sharding import PartitionSpec as P
+from jax.lax import axis_index, axis_size, ppermute
 
 HEADS = 16
 BLK = 128
 ROW = 4
+
+
+def deliver_things_on(local_array, dimension_no):
+    sides = []
+    fan = axis_size("seq")
+    k = 0
+    while k < fan:
+        sides.append((k, (k + 1) % fan))
+        k = k + 1
+    rows = []
+    k = 0
+    while k < fan:
+        rows.append((k, (k - 1) % fan))
+        k += 1
+    left_arr, response = ([local_array], [local_array])
+    for _ in range(fan // 2):
+        front = ppermute(left_arr[-1], "seq", sides)
+        left_arr.append(front)
+    nth = 0
+    while nth < (fan - 1) // 2:
+        opened = ppermute(response[-1], "seq", rows)
+        response.append(opened)
+        nth += 1
+    fresh = jnp.concatenate([*left_arr[::-1], *response[1:]], axis=dimension_no)
+    value_now = axis_index("seq")
+    return jnp.roll(
+        fresh, shift=(value_now - fan // 2) * local_array.shape[dimension_no], axis=dimension_no
+    )
+
+
+fit_the_lanes = functools.partial(deliver_things_on, dimension_no=1)
 
 
 def from_behind(block, axis, distance):
@@ -132,10 +165,7 @@
     section_index = lax.axis_index("section")
     device = lax.axis_index("seq")
     ticks = graphs + sections - 1
-    up_whole, down_whole = (
-        lax.all_gather(w_up, "seq", axis=1, tiled=True),
-        lax.all_gather(w_down, "seq", axis=1, tiled=True),
-    )
+    up_whole, down_whole = (fit_the_lanes(w_up), lax.all_gather(w_down, "seq", axis=1, tiled=True))
     results = jnp.zeros((1, graphs, tok_rows, width), jnp.bfloat16)
     incoming = jnp.zeros((tok_rows, width), jnp.bfloat16)
     for tick_index in range(ticks):

time: 491 us -> 564 us (1.15)
  starting transfers between devices: 46.8 us -> 120 us
  waiting for transfers between devices: 342 us -> 303 us
  local copies, waits for them, and re-layouts: 45.5 us -> 80.2 us
    ppermute x0 -> x15, waiting for transfers between devices: none -> 153 us  [the longest x8 133 us: deliver_things_on(): front = ppermute(left_arr[-1], 'seq', sides)]
    all_gather x1, waiting for transfers between devices: 114 us -> 0.01 us  [local(): lax.all_gather(w_down, 'seq', axis=1, tiled=True)]
    all_gather x1 -> x0, waiting for transfers between devices: 67.9 us -> none  [local(): lax.all_gather(w_up, 'seq', axis=1, tiled=True)]
    ppermute x17, starting transfers between devices: 46.7 us -> 89.3 us  [from_behind(): return lax.ppermute(block, axis, route)]
    ppermute x0 -> x15, starting transfers between devices: none -> 30.8 us  [the longest x7 17.7 us: deliver_things_on(): opened = ppermute(response[-1], 'seq', rows)]
    unnamed x30 -> x69, local copies, waits for them, and re-layouts: 19.1 us -> 45.3 us
    ppermute x17, waiting for transfers between devices: 159 us -> 149 us  [from_behind(): return lax.ppermute(block, axis, route)]
    dynamic_slice x0 -> x1, local copies, waits for them, and re-layouts: none -> 7.63 us  [deliver_things_on(): jnp.roll(fresh, shift=(value_now - fan // 2) * local_array.shape[dimensio...]
  transfers between devices with their start and end apart: 19 -> 33, of which waited for: 11 -> 18; matrix products, arithmetic and copies ran while one was open for 4% -> 10% of each run, Pallas kernels for 0% -> 0%
where the time goes in v1:
time: 564 us; the launch traced here: 559 us
  waiting for transfers between devices  303 us (54%)
  starting transfers between devices  120 us (21%)
  local copies, waits for them, and re-layouts  80.2 us (14%)
  matrix products  26.8 us (5%)
  other arithmetic  14.5 us (3%)
  between operations  13.8 us (2%)
    ppermute x17, waiting for transfers between devices, from_behind(): return lax.ppermute(block, axis, route)  149 us
    ppermute x8, waiting for transfers between devices, deliver_things_on(): front = ppermute(left_arr[-1], 'seq', sides)  133 us
    ppermute x17, starting transfers between devices, from_behind(): return lax.ppermute(block, axis, route)  89.3 us
    unnamed x69, local copies, waits for them, and re-layouts  45.3 us
    ppermute x7, waiting for transfers between devices, deliver_things_on(): opened = ppermute(response[-1], 'seq', rows)  20.5 us
    ppermute x7, starting transfers between devices, deliver_things_on(): opened = ppermute(response[-1], 'seq', rows)  17.7 us
    another operation x6, local copies, waits for them, and re-layouts  13.1 us
    ppermute x8, starting transfers between devices, deliver_things_on(): front = ppermute(left_arr[-1], 'seq', sides)  13.1 us
  transfers between devices with their start and end apart: 33, of which 18 were waited for; matrix products, arithmetic and copies ran while one was open for 10% of the time, Pallas kernels for 0%

profile of v1, /device:TPU:9, one launch (start us, length us, event | category | flops | bytes accessed | tf_op | source)
XLA Modules:
  0.0 559.2 jit_solution(14230796858118847641)
XLA Ops:
  8.5 13.6 %collective-permute-done.8 = bf16[1,256,1024]{2,1,0:T(8,128)(2,1)S(1)} collective-permute-done((bf16[1,256,1024]{2,1,0:T(8,128)(2,1)}, bf16[1,256,1024]{2,1,0:T(8,128)(2,1)S(1)}, u32[]{:S(2)}, u32[]{:S(2)}) %collective-permute-start.8) | collective-permute-done | bytes 524320 | tf_op jit(solution)/shard_map/ppermute | solution.py:28
  22.1 3.3 collective-permute-start.16
  25.4 21.2 %collective-permute-done.9 = bf16[1,256,1024]{2,1,0:T(8,128)(2,1)S(1)} collective-permute-done((bf16[1,256,1024]{2,1,0:T(8,128)(2,1)S(1)}, bf16[1,256,1024]{2,1,0:T(8,128)(2,1)S(1)}, u32[]{:S(2)}, u32[]{:S(2)}) %collective-permute-start.9) | collective-permute-done | bytes 524320 | tf_op jit(solution)/shard_map/ppermute | solution.py:28
  46.6 2.3 collective-permute-start.10
  50.0 32.5 %collective-permute-done.10 = bf16[1,256,1024]{2,1,0:T(8,128)(2,1)} collective-permute-done((bf16[1,256,1024]{2,1,0:T(8,128)(2,1)S(1)}, bf16[1,256,1024]{2,1,0:T(8,128)(2,1)}, u32[]{:S(2)}, u32[]{:S(2)}) %collective-permute-start.10) | collective-permute-done | bytes 524320 | tf_op jit(solution)/shard_map/ppermute | solution.py:28
  82.5 2.3 collective-permute-start.11
  86.7 3.6 collective-permute-start
  90.4 2.3 collective-permute-start.1
  92.7 4.0 collective-permute-start.2
  98.0 16.0 %collective-permute-done.11 = bf16[1,256,1024]{2,1,0:T(8,128)(2,1)} collective-permute-done((bf16[1,256,1024]{2,1,0:T(8,128)(2,1)}, bf16[1,256,1024]{2,1,0:T(8,128)(2,1)}, u32[]{:S(2)}, u32[]{:S(2)}) %collective-permute-start.11) | collective-permute-done | bytes 524320 | tf_op jit(solution)/shard_map/ppermute | solution.py:28
  114.0 2.8 collective-permute-start.12
  119.8 19.1 %collective-permute-start.4 = (bf16[1,128,2048]{2,1,0:T(8,128)(2,1)}, bf16[1,128,2048]{2,1,0:T(8,128)(2,1)S(1)}, u32[]{:S(2)}, u32[]{:S(2)}) collective-permute-start(bf16[1,128,2048]{2,1,0:T(8,128)(2,1)} %get-tuple-element.130), channel_id=1, source_target_pairs={{1,0},{2,1},{3,2},{4,3},{5,4},{6,5},{7,6},{8,7},{9,8},{10,9},{11,1... | collective-permute-start | bytes 1572872 | tf_op jit(solution)/shard_map/ppermute | solution.py:48
  139.0 8.5 %collective-permute-done.2 = bf16[1,128,2048]{2,1,0:T(8,128)(2,1)S(1)} collective-permute-done((bf16[1,128,2048]{2,1,0:T(8,128)(2,1)}, bf16[1,128,2048]{2,1,0:T(8,128)(2,1)S(1)}, u32[]{:S(2)}, u32[]{:S(2)}) %collective-permute-start.2) | collective-permute-done | bytes 524320 | tf_op jit(solution)/shard_map/ppermute | solution.py:48
  149.4 12.1 %collective-permute-start.19 = (bf16[1,256,1024]{2,1,0:T(8,128)(2,1)S(1)}, bf16[1,256,1024]{2,1,0:T(8,128)(2,1)S(1)}, u32[]{:S(2)}, u32[]{:S(2)}) collective-permute-start(bf16[1,256,1024]{2,1,0:T(8,128)(2,1)S(1)} %collective-permute-done.18), channel_id=1, source_target_pairs={{0,15},{1,0},{2,1},{3,2},{4,3},{5,4},{6,5},{7,6},{8,7},{9,8},{10,9... | collective-permute-start | bytes 1572872 | tf_op jit(solution)/shard_map/ppermute | solution.py:32
  161.5 19.1 %collective-permute-done.12 = bf16[1,256,1024]{2,1,0:T(8,128)(2,1)S(1)} collective-permute-done((bf16[1,256,1024]{2,1,0:T(8,128)(2,1)}, bf16[1,256,1024]{2,1,0:T(8,128)(2,1)S(1)}, u32[]{:S(2)}, u32[]{:S(2)}) %collective-permute-start.12) | collective-permute-done | bytes 524320 | tf_op jit(solution)/shard_map/ppermute | solution.py:28
  180.7 21.4 %collective-permute-done.3 = bf16[1,128,2048]{2,1,0:T(8,128)(2,1)S(1)} collective-permute-done((bf16[1,128,2048]{2,1,0:T(8,128)(2,1)}, bf16[1,128,2048]{2,1,0:T(8,128)(2,1)S(1)}, u32[]{:S(2)}, u32[]{:S(2)}) %collective-permute-start.3) | collective-permute-done | bytes 524320 | tf_op jit(solution)/shard_map/ppermute | solution.py:48
  202.1 5.9 %collective-permute-start.6 = (bf16[1,128,2048]{2,1,0:T(8,128)(2,1)}, bf16[1,128,2048]{2,1,0:T(8,128)(2,1)S(1)}, u32[]{:S(2)}, u32[]{:S(2)}) collective-permute-start(bf16[1,128,2048]{2,1,0:T(8,128)(2,1)} %get-tuple-element.130), channel_id=1, source_target_pairs={{4,0},{5,1},{6,2},{7,3},{8,4},{9,5},{10,6},{11,7},{12,8},{13,9},{1... | collective-permute-start | bytes 1572872 | tf_op jit(solution)/shard_map/ppermute | solution.py:48
  208.0 8.8 %collective-permute-done.19 = bf16[1,256,1024]{2,1,0:T(8,128)(2,1)S(1)} collective-permute-done((bf16[1,256,1024]{2,1,0:T(8,128)(2,1)S(1)}, bf16[1,256,1024]{2,1,0:T(8,128)(2,1)S(1)}, u32[]{:S(2)}, u32[]{:S(2)}) %collective-permute-start.19) | collective-permute-done | bytes 524320 | tf_op jit(solution)/shard_map/ppermute | solution.py:32
  216.8 8.7 %collective-permute-done.13 = bf16[1,256,1024]{2,1,0:T(8,128)(2,1)S(1)} collective-permute-done((bf16[1,256,1024]{2,1,0:T(8,128)(2,1)S(1)}, bf16[1,256,1024]{2,1,0:T(8,128)(2,1)S(1)}, u32[]{:S(2)}, u32[]{:S(2)}) %collective-permute-start.13) | collective-permute-done | bytes 524320 | tf_op jit(solution)/shard_map/ppermute | solution.py:28
  225.5 2.2 collective-permute-start.14
  230.4 8.9 %collective-permute-done.20 = bf16[1,256,1024]{2,1,0:T(8,128)(2,1)S(1)} collective-permute-done((bf16[1,256,1024]{2,1,0:T(8,128)(2,1)S(1)}, bf16[1,256,1024]{2,1,0:T(8,128)(2,1)S(1)}, u32[]{:S(2)}, u32[]{:S(2)}) %collective-permute-start.20) | collective-permute-done | bytes 524320 | tf_op jit(solution)/shard_map/ppermute | solution.py:32
  239.3 10.0 %collective-permute-done.14 = bf16[1,256,1024]{2,1,0:T(8,128)(2,1)S(1)} collective-permute-done((bf16[1,256,1024]{2,1,0:T(8,128)(2,1)S(1)}, bf16[1,256,1024]{2,1,0:T(8,128)(2,1)S(1)}, u32[]{:S(2)}, u32[]{:S(2)}) %collective-permute-start.14) | collective-permute-done | bytes 524320 | tf_op jit(solution)/shard_map/ppermute | solution.py:28
  249.3 2.2 collective-permute-start.15
  251.6 18.5 %collective-permute-done.7 = bf16[1,128,2048]{2,1,0:T(8,128)(2,1)S(1)} collective-permute-done((bf16[1,128,2048]{2,1,0:T(8,128)(2,1)}, bf16[1,128,2048]{2,1,0:T(8,128)(2,1)S(1)}, u32[]{:S(2)}, u32[]{:S(2)}) %collective-permute-start.7) | collective-permute-done | bytes 524320 | tf_op jit(solution)/shard_map/ppermute | solution.py:48
  270.1 2.8 collective-permute-done.21
  273.0 11.4 %collective-permute-done.15 = bf16[1,256,1024]{2,1,0:T(8,128)(2,1)S(1)} collective-permute-done((bf16[1,256,1024]{2,1,0:T(8,128)(2,1)S(1)}, bf16[1,256,1024]{2,1,0:T(8,128)(2,1)S(1)}, u32[]{:S(2)}, u32[]{:S(2)}) %collective-permute-start.15) | collective-permute-done | bytes 524320 | tf_op jit(solution)/shard_map/ppermute | solution.py:28
  319.6 7.6 %constant_dynamic-slice_fusion = bf16[1,4096,1024]{2,1,0:T(8,128)(2,1)} fusion(bf16[1,8192,1024]{2,1,0:T(8,128)(2,1)} %constant_dynamic-update-slice_fusion.9, s32[]{:T(128)S(6)} %select_n.71), kind=kLoop, calls=%fused_computation.199 | loop fusion | bytes 16777220 | tf_op jit(solution)/shard_map/jit(_roll_dynamic)/dynamic_slice | solution.py:37
  328.9 61.1 %collective-permute-done.23 = bf16[128,1024]{1,0:T(8,128)(2,1)S(1)} collective-permute-done((bf16[128,1024]{1,0:T(8,128)(2,1)S(1)}, bf16[128,1024]{1,0:T(8,128)(2,1)S(1)}, u32[]{:S(2)}, u32[]{:S(2)}) %collective-permute-start.23) | collective-permute-done | bytes 262176 | tf_op jit(solution)/shard_map/ppermute | solution.py:48
  391.0 5.0 conditional.6
  391.1 2.2 fusion.30
  393.4 2.1 fusion.33
  396.0 25.2 %collective-permute-start.24 = (bf16[1,128,2048]{2,1,0:T(8,128)(2,1)S(1)}, bf16[1,128,2048]{2,1,0:T(8,128)(2,1)S(1)}, u32[]{:S(2)}, u32[]{:S(2)}) collective-permute-start(bf16[1,128,2048]{2,1,0:T(8,128)(2,1)S(1)} %get-tuple-element.132), channel_id=1, source_target_pairs={{0,5},{1,6},{2,7},{3,8},{4,9},{5,10},{6,11},{7,12},{8,13},{9,14},{... | collective-permute-start | bytes 1572872 | tf_op jit(solution)/shard_map/ppermute | solution.py:48
  423.2 8.5 %collective-permute-start.26 = (bf16[1,128,2048]{2,1,0:T(8,128)(2,1)S(1)}, bf16[1,128,2048]{2,1,0:T(8,128)(2,1)S(1)}, u32[]{:S(2)}, u32[]{:S(2)}) collective-permute-start(bf16[1,128,2048]{2,1,0:T(8,128)(2,1)S(1)} %get-tuple-element.132), channel_id=1, source_target_pairs={{0,3},{1,4},{2,5},{3,6},{4,7},{5,8},{6,9},{7,10},{8,11},{9,12},{10... | collective-permute-start | bytes 1572872 | tf_op jit(solution)/shard_map/ppermute | solution.py:48
  433.6 5.2 collective-permute-start.28
  444.3 23.7 %collective-permute-done.26 = bf16[1,128,2048]{2,1,0:T(8,128)(2,1)S(1)} collective-permute-done((bf16[1,128,2048]{2,1,0:T(8,128)(2,1)S(1)}, bf16[1,128,2048]{2,1,0:T(8,128)(2,1)S(1)}, u32[]{:S(2)}, u32[]{:S(2)}) %collective-permute-start.26) | collective-permute-done | bytes 524320 | tf_op jit(solution)/shard_map/ppermute | solution.py:48
  470.9 13.3 %collective-permute-done.27 = bf16[1,128,2048]{2,1,0:T(8,128)(2,1)S(1)} collective-permute-done((bf16[1,128,2048]{2,1,0:T(8,128)(2,1)S(1)}, bf16[1,128,2048]{2,1,0:T(8,128)(2,1)S(1)}, u32[]{:S(2)}, u32[]{:S(2)}) %collective-permute-start.27) | collective-permute-done | bytes 524320 | tf_op jit(solution)/shard_map/ppermute | solution.py:48
  485.9 2.8 collective-permute-done.28
  493.0 58.6 %conditional.7 = (bf16[128,1024]{1,0:T(8,128)(2,1)S(1)}) conditional(s32[]{:T(128)} %convert_element_type.100, () %tuple.42, (bf16[128,1024]{1,0:T(8,128)(2,1)S(1)}, bf16[11,128,2048]{2,1,0:T(8,128)(2,1)}, s32[]{:T(128)}, s32[1,9]{1,0:T(1,128)S(1)}, s32[1]{0:T(128)}, /*index=5*/bf16[128,1024]{1,0:T(8,128)(2,1)S(1)}, ...), branch_computations={%region_11.13_spmd, %region_12.17_spmd} | conditional | flops 3047426304 | bytes 114586176 | solution.py:207
  493.7 5.2 fusion.164
  498.9 4.1 gather_fusion.2
  503.0 2.3 gather_fusion.3
  505.3 4.3 bitcast_select_fusion.3
  509.6 7.3 %reshape.288 = bf16[1152,16,64]{2,1,0:T(8,128)(2,1)} reshape(bf16[1,9,128,1024]{3,2,1,0:T(8,128)(2,1)} %get-tuple-element.189) | data formatting | bytes 4718592 | tf_op jit(solution)/shard_map/reshape.89
  517.1 3.2 fusion.111
  521.1 6.7 %fusion.165 = (f32[16,128]{1,0:T(8,128)S(1)}, f32[16,128,1152]{1,2,0:T(8,128)}) fusion(f32[16,1152,128]{2,1,0:T(8,128)S(1)} %fusion.111, pred[1152]{0:T(1024)(128)(4,1)S(1)} %broadcast_bitcast_fusion.1), kind=kOutput, calls=%fused_computation.203 | output fusion | flops 14156927 | bytes 18883712 | tf_op jit(solution)/shard_map/cond/branch_1_fun/sub | solution.py:75
  527.7 4.7 reshape.287
  532.5 8.2 %fusion.141 = bf16[16,64,128]{2,1,0:T(8,128)(2,1)S(1)} fusion(f32[16,128,1152]{1,2,0:T(8,128)} %get-tuple-element.191, f32[16,128]{1,0:T(8,128)S(1)} %get-tuple-element.190, bf16[1152,16,64]{2,1,0:T(8,128)(2,1)} %reshape.287), kind=kOutput, calls=%fused_computation.123 | convolution fusion | flops 306839552 | bytes 12066816 | tf_op jit(solution)/shard_map/cond/branch_1_fun/bhqk,bkhd->bqhd/dot_general | solution.py:130
  541.3 10.0 %fusion.138 = bf16[128,1024]{1,0:T(8,128)(2,1)S(1)} fusion(f32[128,1024]{1,0:T(8,128)S(1)} %get-tuple-element.193, bf16[1,4096,1024]{2,1,0:T(8,128)(2,1)} %get-tuple-element.125, bf16[1,4096,1024]{2,1,0:T(8,128)(2,1)} %get-tuple-element.124, f32[1024]{0:T(1024)S(1)} %bitcast.180, f32[128]{0:T(128)S(1)} %add_rsqrt_fusion.3), kind=kOutput, calls=%fused_computation.122 | convolution fusion | flops 2152857600 | bytes 17568256 | tf_op jit(solution)/shard_map/cond/branch_1_fun/dot_general | solution.py:144
  (133 shorter events, 74.5 us)
Async XLA Ops:
  6.5 320.7 %all-gather.2.cloned.1.call-start = ((), (), s32[]{:S(2)}) async-start(), calls=%async_computation | async-start | bytes 8912896 | tf_op jit(solution)/shard_map/all_gather | solution.py:168
  7.3 14.9 %collective-permute-start.8 = (bf16[1,256,1024]{2,1,0:T(8,128)(2,1)}, bf16[1,256,1024]{2,1,0:T(8,128)(2,1)S(1)}, u32[]{:S(2)}, u32[]{:S(2)}) collective-permute-start(bf16[1,256,1024]{2,1,0:T(8,128)(2,1)} %param.33), channel_id=1, source_target_pairs={{0,1},{1,2},{2,3},{3,4},{4,5},{5,6},{6,7},{7,8},{8,9},{9,10},{10,1... | collective-permute-start | bytes 1572872 | tf_op jit(solution)/shard_map/ppermute | solution.py:28
  22.1 24.5 %collective-permute-start.9 = (bf16[1,256,1024]{2,1,0:T(8,128)(2,1)S(1)}, bf16[1,256,1024]{2,1,0:T(8,128)(2,1)S(1)}, u32[]{:S(2)}, u32[]{:S(2)}) collective-permute-start(bf16[1,256,1024]{2,1,0:T(8,128)(2,1)S(1)} %collective-permute-done.8), channel_id=1, source_target_pairs={{0,1},{1,2},{2,3},{3,4},{4,5},{5,6},{6,7},{7,8},{8,9},{9,10},{10,1... | collective-permute-start | bytes 1572872 | tf_op jit(solution)/shard_map/ppermute | solution.py:28
  22.1 26.8 %collective-permute-start.16 = (bf16[1,256,1024]{2,1,0:T(8,128)(2,1)}, bf16[1,256,1024]{2,1,0:T(8,128)(2,1)}, u32[]{:S(2)}, u32[]{:S(2)}) collective-permute-start(bf16[1,256,1024]{2,1,0:T(8,128)(2,1)} %param.33), channel_id=1, source_target_pairs={{0,15},{1,0},{2,1},{3,2},{4,3},{5,4},{6,5},{7,6},{8,7},{9,8},{10,9... | collective-permute-start | bytes 1572872 | tf_op jit(solution)/shard_map/ppermute | solution.py:32
  46.6 39.2 %copy-start.6 = (bf16[1,256,1024]{2,1,0:T(8,128)(2,1)}, bf16[1,256,1024]{2,1,0:T(8,128)(2,1)S(1)}, u32[]{:S(2)}) copy-start(bf16[1,256,1024]{2,1,0:T(8,128)(2,1)S(1)} %collective-permute-done.9) | copy-start | bytes 1572868
  46.6 35.9 %collective-permute-start.10 = (bf16[1,256,1024]{2,1,0:T(8,128)(2,1)S(1)}, bf16[1,256,1024]{2,1,0:T(8,128)(2,1)}, u32[]{:S(2)}, u32[]{:S(2)}) collective-permute-start(bf16[1,256,1024]{2,1,0:T(8,128)(2,1)S(1)} %collective-permute-done.9), channel_id=1, source_target_pairs={{0,1},{1,2},{2,3},{3,4},{4,5},{5,6},{6,7},{7,8},{8,9},{9,10},{10,1... | collective-permute-start | bytes 1572872 | tf_op jit(solution)/shard_map/ppermute | solution.py:28
  48.9 47.8 %collective-permute-start.17 = (bf16[1,256,1024]{2,1,0:T(8,128)(2,1)}, bf16[1,256,1024]{2,1,0:T(8,128)(2,1)}, u32[]{:S(2)}, u32[]{:S(2)}) collective-permute-start(bf16[1,256,1024]{2,1,0:T(8,128)(2,1)} %collective-permute-done.16), channel_id=1, source_target_pairs={{0,15},{1,0},{2,1},{3,2},{4,3},{5,4},{6,5},{7,6},{8,7},{9,8},{10,9... | collective-permute-start | bytes 1572872 | tf_op jit(solution)/shard_map/ppermute | solution.py:32
  82.5 31.5 %collective-permute-start.11 = (bf16[1,256,1024]{2,1,0:T(8,128)(2,1)}, bf16[1,256,1024]{2,1,0:T(8,128)(2,1)}, u32[]{:S(2)}, u32[]{:S(2)}) collective-permute-start(bf16[1,256,1024]{2,1,0:T(8,128)(2,1)} %collective-permute-done.10), channel_id=1, source_target_pairs={{0,1},{1,2},{2,3},{3,4},{4,5},{5,6},{6,7},{7,8},{8,9},{9,10},{10,1... | collective-permute-start | bytes 1572872 | tf_op jit(solution)/shard_map/ppermute | solution.py:28
  86.7 30.1 %collective-permute-start = (bf16[1,128,2048]{2,1,0:T(8,128)(2,1)}, bf16[1,128,2048]{2,1,0:T(8,128)(2,1)}, u32[]{:S(2)}, u32[]{:S(2)}) collective-permute-start(bf16[1,128,2048]{2,1,0:T(8,128)(2,1)} %get-tuple-element.130), channel_id=1, source_target_pairs={{0,5},{1,6},{2,7},{3,8},{4,9},{5,10},{6,11},{7,12},{8,13},{9,14},{... | collective-permute-start | bytes 1572872 | tf_op jit(solution)/shard_map/ppermute | solution.py:48
  90.4 29.4 %collective-permute-start.1 = (bf16[1,128,2048]{2,1,0:T(8,128)(2,1)}, bf16[1,128,2048]{2,1,0:T(8,128)(2,1)S(1)}, u32[]{:S(2)}, u32[]{:S(2)}) collective-permute-start(bf16[1,128,2048]{2,1,0:T(8,128)(2,1)} %get-tuple-element.130), channel_id=1, source_target_pairs={{0,4},{1,5},{2,6},{3,7},{4,8},{5,9},{6,10},{7,11},{8,12},{9,13},{1... | collective-permute-start | bytes 1572872 | tf_op jit(solution)/shard_map/ppermute | solution.py:48
  92.7 54.8 %collective-permute-start.2 = (bf16[1,128,2048]{2,1,0:T(8,128)(2,1)}, bf16[1,128,2048]{2,1,0:T(8,128)(2,1)S(1)}, u32[]{:S(2)}, u32[]{:S(2)}) collective-permute-start(bf16[1,128,2048]{2,1,0:T(8,128)(2,1)} %get-tuple-element.130), channel_id=1, source_target_pairs={{0,3},{1,4},{2,5},{3,6},{4,7},{5,8},{6,9},{7,10},{8,11},{9,12},{10... | collective-permute-start | bytes 1572872 | tf_op jit(solution)/shard_map/ppermute | solution.py:48
  96.7 52.7 %collective-permute-start.18 = (bf16[1,256,1024]{2,1,0:T(8,128)(2,1)}, bf16[1,256,1024]{2,1,0:T(8,128)(2,1)S(1)}, u32[]{:S(2)}, u32[]{:S(2)}) collective-permute-start(bf16[1,256,1024]{2,1,0:T(8,128)(2,1)} %collective-permute-done.17), channel_id=1, source_target_pairs={{0,15},{1,0},{2,1},{3,2},{4,3},{5,4},{6,5},{7,6},{8,7},{9,8},{10,9... | collective-permute-start | bytes 1572872 | tf_op jit(solution)/shard_map/ppermute | solution.py:32
  114.0 66.6 %collective-permute-start.12 = (bf16[1,256,1024]{2,1,0:T(8,128)(2,1)}, bf16[1,256,1024]{2,1,0:T(8,128)(2,1)S(1)}, u32[]{:S(2)}, u32[]{:S(2)}) collective-permute-start(bf16[1,256,1024]{2,1,0:T(8,128)(2,1)} %collective-permute-done.11), channel_id=1, source_target_pairs={{0,1},{1,2},{2,3},{3,4},{4,5},{5,6},{6,7},{7,8},{8,9},{9,10},{10,1... | collective-permute-start | bytes 1572872 | tf_op jit(solution)/shard_map/ppermute | solution.py:28
  116.8 85.3 %collective-permute-start.3 = (bf16[1,128,2048]{2,1,0:T(8,128)(2,1)}, bf16[1,128,2048]{2,1,0:T(8,128)(2,1)S(1)}, u32[]{:S(2)}, u32[]{:S(2)}) collective-permute-start(bf16[1,128,2048]{2,1,0:T(8,128)(2,1)} %get-tuple-element.130), channel_id=1, source_target_pairs={{0,1},{1,2},{2,3},{3,4},{4,5},{5,6},{6,7},{7,8},{8,9},{9,10},{10,1... | collective-permute-start | bytes 1572872 | tf_op jit(solution)/shard_map/ppermute | solution.py:48
  119.8 109.0 %collective-permute-start.4 = (bf16[1,128,2048]{2,1,0:T(8,128)(2,1)}, bf16[1,128,2048]{2,1,0:T(8,128)(2,1)S(1)}, u32[]{:S(2)}, u32[]{:S(2)}) collective-permute-start(bf16[1,128,2048]{2,1,0:T(8,128)(2,1)} %get-tuple-element.130), channel_id=1, source_target_pairs={{1,0},{2,1},{3,2},{4,3},{5,4},{6,5},{7,6},{8,7},{9,8},{10,9},{11,1... | collective-permute-start | bytes 1572872 | tf_op jit(solution)/shard_map/ppermute | solution.py:48
  147.5 103.9 %collective-permute-start.5 = (bf16[1,128,2048]{2,1,0:T(8,128)(2,1)}, bf16[1,128,2048]{2,1,0:T(8,128)(2,1)S(1)}, u32[]{:S(2)}, u32[]{:S(2)}) collective-permute-start(bf16[1,128,2048]{2,1,0:T(8,128)(2,1)} %get-tuple-element.130), channel_id=1, source_target_pairs={{3,0},{4,1},{5,2},{6,3},{7,4},{8,5},{9,6},{10,7},{11,8},{12,9},{13... | collective-permute-start | bytes 1572872 | tf_op jit(solution)/shard_map/ppermute | solution.py:48
  149.4 67.3 %collective-permute-start.19 = (bf16[1,256,1024]{2,1,0:T(8,128)(2,1)S(1)}, bf16[1,256,1024]{2,1,0:T(8,128)(2,1)S(1)}, u32[]{:S(2)}, u32[]{:S(2)}) collective-permute-start(bf16[1,256,1024]{2,1,0:T(8,128)(2,1)S(1)} %collective-permute-done.18), channel_id=1, source_target_pairs={{0,15},{1,0},{2,1},{3,2},{4,3},{5,4},{6,5},{7,6},{8,7},{9,8},{10,9... | collective-permute-start | bytes 1572872 | tf_op jit(solution)/shard_map/ppermute | solution.py:32
  180.6 44.9 %collective-permute-start.13 = (bf16[1,256,1024]{2,1,0:T(8,128)(2,1)S(1)}, bf16[1,256,1024]{2,1,0:T(8,128)(2,1)S(1)}, u32[]{:S(2)}, u32[]{:S(2)}) collective-permute-start(bf16[1,256,1024]{2,1,0:T(8,128)(2,1)S(1)} %collective-permute-done.12), channel_id=1, source_target_pairs={{0,1},{1,2},{2,3},{3,4},{4,5},{5,6},{6,7},{7,8},{8,9},{9,10},{10,1... | collective-permute-start | bytes 1572872 | tf_op jit(solution)/shard_map/ppermute | solution.py:28
  202.1 49.4 %collective-permute-start.6 = (bf16[1,128,2048]{2,1,0:T(8,128)(2,1)}, bf16[1,128,2048]{2,1,0:T(8,128)(2,1)S(1)}, u32[]{:S(2)}, u32[]{:S(2)}) collective-permute-start(bf16[1,128,2048]{2,1,0:T(8,128)(2,1)} %get-tuple-element.130), channel_id=1, source_target_pairs={{4,0},{5,1},{6,2},{7,3},{8,4},{9,5},{10,6},{11,7},{12,8},{13,9},{1... | collective-permute-start | bytes 1572872 | tf_op jit(solution)/shard_map/ppermute | solution.py:48
  216.8 22.5 %collective-permute-start.20 = (bf16[1,256,1024]{2,1,0:T(8,128)(2,1)S(1)}, bf16[1,256,1024]{2,1,0:T(8,128)(2,1)S(1)}, u32[]{:S(2)}, u32[]{:S(2)}) collective-permute-start(bf16[1,256,1024]{2,1,0:T(8,128)(2,1)S(1)} %collective-permute-done.19), channel_id=1, source_target_pairs={{0,15},{1,0},{2,1},{3,2},{4,3},{5,4},{6,5},{7,6},{8,7},{9,8},{10,9... | collective-permute-start | bytes 1572872 | tf_op jit(solution)/shard_map/ppermute | solution.py:32
  225.5 23.7 %collective-permute-start.14 = (bf16[1,256,1024]{2,1,0:T(8,128)(2,1)S(1)}, bf16[1,256,1024]{2,1,0:T(8,128)(2,1)S(1)}, u32[]{:S(2)}, u32[]{:S(2)}) collective-permute-start(bf16[1,256,1024]{2,1,0:T(8,128)(2,1)S(1)} %collective-permute-done.13), channel_id=1, source_target_pairs={{0,1},{1,2},{2,3},{3,4},{4,5},{5,6},{6,7},{7,8},{8,9},{9,10},{10,1... | collective-permute-start | bytes 1572872 | tf_op jit(solution)/shard_map/ppermute | solution.py:28
  228.8 62.7 %copy-start.7 = (bf16[1,256,1024]{2,1,0:T(8,128)(2,1)S(1)}, bf16[1,256,1024]{2,1,0:T(8,128)(2,1)}, u32[]{:S(2)}) copy-start(bf16[1,256,1024]{2,1,0:T(8,128)(2,1)} %copy-done.6) | copy-start | bytes 1572868
  228.8 41.2 %collective-permute-start.7 = (bf16[1,128,2048]{2,1,0:T(8,128)(2,1)}, bf16[1,128,2048]{2,1,0:T(8,128)(2,1)S(1)}, u32[]{:S(2)}, u32[]{:S(2)}) collective-permute-start(bf16[1,128,2048]{2,1,0:T(8,128)(2,1)} %get-tuple-element.130), channel_id=1, source_target_pairs={{5,0},{6,1},{7,2},{8,3},{9,4},{10,5},{11,6},{12,7},{13,8},{14,9},{... | collective-permute-start | bytes 1572872 | tf_op jit(solution)/shard_map/ppermute | solution.py:48
  230.4 62.8 %copy-start.5 = (bf16[1,256,1024]{2,1,0:T(8,128)(2,1)S(1)}, bf16[1,256,1024]{2,1,0:T(8,128)(2,1)}, u32[]{:S(2)}) copy-start(bf16[1,256,1024]{2,1,0:T(8,128)(2,1)} %param.33) | copy-start | bytes 1572868
  239.3 33.7 %collective-permute-start.21 = (bf16[1,256,1024]{2,1,0:T(8,128)(2,1)S(1)}, bf16[1,256,1024]{2,1,0:T(8,128)(2,1)S(1)}, u32[]{:S(2)}, u32[]{:S(2)}) collective-permute-start(bf16[1,256,1024]{2,1,0:T(8,128)(2,1)S(1)} %collective-permute-done.20), channel_id=1, source_target_pairs={{0,15},{1,0},{2,1},{3,2},{4,3},{5,4},{6,5},{7,6},{8,7},{9,8},{10,9... | collective-permute-start | bytes 1572872 | tf_op jit(solution)/shard_map/ppermute | solution.py:32
  249.3 35.1 %collective-permute-start.15 = (bf16[1,256,1024]{2,1,0:T(8,128)(2,1)S(1)}, bf16[1,256,1024]{2,1,0:T(8,128)(2,1)S(1)}, u32[]{:S(2)}, u32[]{:S(2)}) collective-permute-start(bf16[1,256,1024]{2,1,0:T(8,128)(2,1)S(1)} %collective-permute-done.14), channel_id=1, source_target_pairs={{0,1},{1,2},{2,3},{3,4},{4,5},{5,6},{6,7},{7,8},{8,9},{9,10},{10,1... | collective-permute-start | bytes 1572872 | tf_op jit(solution)/shard_map/ppermute | solution.py:28
  270.1 27.6 %copy-start.4 = (bf16[11,128,2048]{2,1,0:T(8,128)(2,1)}, bf16[11,128,2048]{2,1,0:T(8,128)(2,1)S(1)}, u32[]{:S(2)}) copy-start(bf16[11,128,2048]{2,1,0:T(8,128)(2,1)S(1)} %constant_dynamic-update-slice_fusion) | copy-start | bytes 17301508
  273.0 28.1 %collective-permute-start.22 = (bf16[1,256,1024]{2,1,0:T(8,128)(2,1)S(1)}, bf16[1,256,1024]{2,1,0:T(8,128)(2,1)S(1)}, u32[]{:S(2)}, u32[]{:S(2)}) collective-permute-start(bf16[1,256,1024]{2,1,0:T(8,128)(2,1)S(1)} %collective-permute-done.21), channel_id=1, source_target_pairs={{0,15},{1,0},{2,1},{3,2},{4,3},{5,4},{6,5},{7,6},{8,7},{9,8},{10,9... | collective-permute-start | bytes 1572872 | tf_op jit(solution)/shard_map/ppermute | solution.py:32
  319.6 7.6 %copy-start.14 = (s32[1,9]{1,0:T(1,128)S(1)}, s32[1,9]{1,0:T(1,128)}, u32[]{:S(2)}) copy-start(s32[1,9]{1,0:T(1,128)} %param.26) | copy-start | bytes 112
  319.6 7.6 %copy-start.15 = (f32[1,1024]{1,0:T(1,128)S(1)}, f32[1,1024]{1,0:T(1,128)}, u32[]{:S(2)}) copy-start(f32[1,1024]{1,0:T(1,128)} %param.35) | copy-start | bytes 12292
  327.3 63.7 %copy-start.12 = (f32[1,1024]{1,0:T(1,128)S(1)}, f32[1,1024]{1,0:T(1,128)}, u32[]{:S(2)}) copy-start(f32[1,1024]{1,0:T(1,128)} %param.32) | copy-start | bytes 12292
  327.5 63.4 %copy-start.8 = (bf16[128,1024]{1,0:T(8,128)(2,1)}, bf16[128,1024]{1,0:T(8,128)(2,1)S(1)}, u32[]{:S(2)}) copy-start(bf16[128,1024]{1,0:T(8,128)(2,1)S(1)} %get-tuple-element.202) | copy-start | bytes 786436
  327.5 62.4 %collective-permute-start.23 = (bf16[128,1024]{1,0:T(8,128)(2,1)S(1)}, bf16[128,1024]{1,0:T(8,128)(2,1)S(1)}, u32[]{:S(2)}, u32[]{:S(2)}) collective-permute-start(bf16[128,1024]{1,0:T(8,128)(2,1)S(1)} %get-tuple-element.202), channel_id=1, source_target_pairs={{0,16},{1,17},{2,18},{3,19},{4,20},{5,21},{6,22},{7,23},{8,24},{9,... | collective-permute-start | bytes 786440 | tf_op jit(solution)/shard_map/ppermute | solution.py:48
  391.0 4.5 copy-start.1
  396.0 42.7 %collective-permute-start.24 = (bf16[1,128,2048]{2,1,0:T(8,128)(2,1)S(1)}, bf16[1,128,2048]{2,1,0:T(8,128)(2,1)S(1)}, u32[]{:S(2)}, u32[]{:S(2)}) collective-permute-start(bf16[1,128,2048]{2,1,0:T(8,128)(2,1)S(1)} %get-tuple-element.132), channel_id=1, source_target_pairs={{0,5},{1,6},{2,7},{3,8},{4,9},{5,10},{6,11},{7,12},{8,13},{9,14},{... | collective-permute-start | bytes 1572872 | tf_op jit(solution)/shard_map/ppermute | solution.py:48
  421.2 20.3 %collective-permute-start.25 = (bf16[1,128,2048]{2,1,0:T(8,128)(2,1)S(1)}, bf16[1,128,2048]{2,1,0:T(8,128)(2,1)S(1)}, u32[]{:S(2)}, u32[]{:S(2)}) collective-permute-start(bf16[1,128,2048]{2,1,0:T(8,128)(2,1)S(1)} %get-tuple-element.132), channel_id=1, source_target_pairs={{0,4},{1,5},{2,6},{3,7},{4,8},{5,9},{6,10},{7,11},{8,12},{9,13},{1... | collective-permute-start | bytes 1572872 | tf_op jit(solution)/shard_map/ppermute | solution.py:48
  423.2 44.8 %collective-permute-start.26 = (bf16[1,128,2048]{2,1,0:T(8,128)(2,1)S(1)}, bf16[1,128,2048]{2,1,0:T(8,128)(2,1)S(1)}, u32[]{:S(2)}, u32[]{:S(2)}) collective-permute-start(bf16[1,128,2048]{2,1,0:T(8,128)(2,1)S(1)} %get-tuple-element.132), channel_id=1, source_target_pairs={{0,3},{1,4},{2,5},{3,6},{4,7},{5,8},{6,9},{7,10},{8,11},{9,12},{10... | collective-permute-start | bytes 1572872 | tf_op jit(solution)/shard_map/ppermute | solution.py:48
  431.6 52.6 %collective-permute-start.27 = (bf16[1,128,2048]{2,1,0:T(8,128)(2,1)S(1)}, bf16[1,128,2048]{2,1,0:T(8,128)(2,1)S(1)}, u32[]{:S(2)}, u32[]{:S(2)}) collective-permute-start(bf16[1,128,2048]{2,1,0:T(8,128)(2,1)S(1)} %get-tuple-element.132), channel_id=1, source_target_pairs={{0,1},{1,2},{2,3},{3,4},{4,5},{5,6},{6,7},{7,8},{8,9},{9,10},{10,1... | collective-permute-start | bytes 1572872 | tf_op jit(solution)/shard_map/ppermute | solution.py:48
  433.6 55.2 %collective-permute-start.28 = (bf16[1,128,2048]{2,1,0:T(8,128)(2,1)S(1)}, bf16[1,128,2048]{2,1,0:T(8,128)(2,1)S(1)}, u32[]{:S(2)}, u32[]{:S(2)}) collective-permute-start(bf16[1,128,2048]{2,1,0:T(8,128)(2,1)S(1)} %get-tuple-element.132), channel_id=1, source_target_pairs={{1,0},{2,1},{3,2},{4,3},{5,4},{6,5},{7,6},{8,7},{9,8},{10,9},{11,1... | collective-permute-start | bytes 1572872 | tf_op jit(solution)/shard_map/ppermute | solution.py:48
  438.8 51.7 %collective-permute-start.29 = (bf16[1,128,2048]{2,1,0:T(8,128)(2,1)S(1)}, bf16[1,128,2048]{2,1,0:T(8,128)(2,1)S(1)}, u32[]{:S(2)}, u32[]{:S(2)}) collective-permute-start(bf16[1,128,2048]{2,1,0:T(8,128)(2,1)S(1)} %get-tuple-element.132), channel_id=1, source_target_pairs={{3,0},{4,1},{5,2},{6,3},{7,4},{8,5},{9,6},{10,7},{11,8},{12,9},{13... | collective-permute-start | bytes 1572872 | tf_op jit(solution)/shard_map/ppermute | solution.py:48
  441.5 49.8 %collective-permute-start.30 = (bf16[1,128,2048]{2,1,0:T(8,128)(2,1)S(1)}, bf16[1,128,2048]{2,1,0:T(8,128)(2,1)S(1)}, u32[]{:S(2)}, u32[]{:S(2)}) collective-permute-start(bf16[1,128,2048]{2,1,0:T(8,128)(2,1)S(1)} %get-tuple-element.132), channel_id=1, source_target_pairs={{4,0},{5,1},{6,2},{7,3},{8,4},{9,5},{10,6},{11,7},{12,8},{13,9},{1... | collective-permute-start | bytes 1572872 | tf_op jit(solution)/shard_map/ppermute | solution.py:48
  468.0 24.1 %collective-permute-start.31 = (bf16[1,128,2048]{2,1,0:T(8,128)(2,1)S(1)}, bf16[1,128,2048]{2,1,0:T(8,128)(2,1)S(1)}, u32[]{:S(2)}, u32[]{:S(2)}) collective-permute-start(bf16[1,128,2048]{2,1,0:T(8,128)(2,1)S(1)} %get-tuple-element.132), channel_id=1, source_target_pairs={{5,0},{6,1},{7,2},{8,3},{9,4},{10,5},{11,6},{12,7},{13,8},{14,9},{... | collective-permute-start | bytes 1572872 | tf_op jit(solution)/shard_map/ppermute | solution.py:48
  493.0 58.7 %copy-start.9 = (bf16[128,1024]{1,0:T(8,128)(2,1)S(1)}, bf16[128,1024]{1,0:T(8,128)(2,1)}, u32[]{:S(2)}) copy-start(bf16[128,1024]{1,0:T(8,128)(2,1)} %copy-done.8) | copy-start | bytes 786436
  493.0 0.7 copy-start.10
  509.6 7.3 %copy-start.11 = (bf16[128,1024]{1,0:T(8,128)(2,1)S(1)}, bf16[128,1024]{1,0:T(8,128)(2,1)}, u32[]{:S(2)}) copy-start(bf16[128,1024]{1,0:T(8,128)(2,1)} %copy-done.10) | copy-start | bytes 786436 | tf_op jit(solution)/shard_map/cond
  532.5 8.2 %copy-start.3 = (bf16[1,1024,1024]{2,1,0:T(8,128)(2,1)S(1)}, bf16[1,1024,1024]{2,1,0:T(8,128)(2,1)}, u32[]{:S(2)}) copy-start(bf16[1,1024,1024]{2,1,0:T(8,128)(2,1)} %get-tuple-element.122) | copy-start | bytes 6291460 | tf_op jit(solution)/shard_map/cond
Sparse Core Ops, SparseCore 0:
  10.1 200.1 all-gather.1
